TPU v7x, 32 devices: a whole 2x2x4 slice. The times are simulated.
32 devices in a mesh: pop: 16 (over z, y, core), tp: 2 (over x).
Axes of the slice: x: 2, y: 2, z: 4, core: 2. Of those that a mesh axis runs over, the one named last changes fastest.
Arguments:
- tokens: bfloat16 [16, 512, 1792], P('pop', None, 'tp'), may hold values from -6 to 6
- weight: bfloat16 [16, 1792, 7168], P('pop', 'tp'), may hold values from -0.125 to 0.125
- momentum: bfloat16 [16, 1792, 7168], P('pop', 'tp'), may hold values from -6 to 6
- cotangent: bfloat16 [16, 512, 7168], P('pop', None, 'tp'), may hold values from -0.5 to 0.5
- assignment: int32 [4, 2], replicated, may hold values from 0 to 15, as said below
- lr_index: int32 [16], replicated, may hold values from 0 to 7
- rates: float32 [8], replicated, may hold values from 0.01 to 0.1
Outputs:
- activation: bfloat16 [16, 512, 7168], P('pop', None, 'tp')
- new_weight: bfloat16 [16, 1792, 7168], P('pop', 'tp')
Inputs may be any that keep to these rules, and one draw needn't show every extreme that they name: `assignment`: column 0 names 4 distinct members; column 1 names exactly 1 distinct members, each in some row, none of them in column 0.
All inputs are finite; a program needn't handle non-finite values.
Results may differ from a plain program's by a relative error of at most 0.015.
Values may be sent and summed in bfloat16 or wider, within the bound.
A program may use at most 192 MiB of HBM per device.

v0:
```python
import jax
import jax.numpy as jnp
from jax import lax
from jax.sharding import PartitionSpec as P


def from_root(value, axis, source):
    kept = jnp.where(lax.axis_index(axis) == source, value, 0).astype(value.dtype)
    return lax.psum(kept, axis)


def gelu_tanh(value):
    return jax.nn.gelu(value, approximate=True)


def activate(hidden, cot_block):
    active, pullback = jax.vjp(gelu_tanh, hidden)
    grad_hidden = pullback(cot_block.astype(jnp.float32))[0].astype(jnp.bfloat16)
    return (active.astype(jnp.bfloat16), grad_hidden)


def local(tokens, weight, momentum, cotangent, assignment, lr_index, rates):
    members = lax.axis_size("pop")
    me = lax.axis_index("pop")
    member_ids = jnp.arange(members, dtype=jnp.int32)
    hit = assignment[:, 0][None, :] == member_ids[:, None]
    source_all = jnp.where(
        jnp.any(hit, axis=1),
        jnp.sum(jnp.where(hit, assignment[:, 1][None, :], 0), axis=1),
        member_ids,
    )
    my_source = jnp.sum(jnp.where(member_ids == me, source_all, 0))
    my_index = jnp.sum(jnp.where(member_ids == me, lr_index, 0))
    rate_ids = jnp.arange(rates.shape[0], dtype=jnp.int32)
    my_rate = jnp.sum(jnp.where(rate_ids == my_index, rates, 0.0))
    tops = assignment.shape[0] // 4
    winner_hit = assignment[:, 1][None, :] == member_ids[:, None]
    present = jnp.any(winner_hit, axis=1)
    roots = jnp.sort(jnp.where(present, member_ids, members))[:tops]
    taken_weight = weight[0]
    taken_momentum = momentum[0]
    for turn in range(tops):
        arrived = (from_root(weight, "pop", roots[turn]), from_root(momentum, "pop", roots[turn]))
        chosen = my_source == roots[turn]
        taken_weight = jnp.where(chosen, arrived[0][0], taken_weight)
        taken_momentum = jnp.where(chosen, arrived[1][0], taken_momentum)
    inputs = tokens[0]
    partial_value = jnp.dot(inputs, taken_weight, preferred_element_type=jnp.float32)
    share_cols = cotangent.shape[2]
    cot_whole = lax.all_gather(cotangent[0], "tp", axis=1, tiled=True)
    hidden = lax.psum(partial_value.astype(jnp.bfloat16), "tp").astype(jnp.float32)
    active_whole, grad_hidden = activate(hidden, cot_whole)
    activation = lax.dynamic_slice_in_dim(
        active_whole, lax.axis_index("tp") * share_cols, share_cols, 1
    )
    grad_weight = lax.dot_general(
        inputs, grad_hidden, (((0,), (0,)), ((), ())), preferred_element_type=jnp.float32
    )
    new_momentum = 0.9 * taken_momentum.astype(jnp.float32) + grad_weight
    updated = (taken_weight.astype(jnp.float32) - my_rate * new_momentum).astype(jnp.bfloat16)
    return (activation[None], updated[None])


def solution(mesh):
    placed = (
        P("pop", None, "tp"),
        P("pop", "tp", None),
        P("pop", "tp", None),
        P("pop", None, "tp"),
        P(),
        P(),
        P(),
    )
    return jax.shard_map(
        local,
        mesh=mesh,
        in_specs=placed,
        out_specs=(P("pop", None, "tp"), P("pop", "tp", None)),
        check_vma=False,
    )
```

profile of v0, /device:TPU:1, one launch (start us, length us, event | category | flops | bytes accessed | tf_op | source)
XLA Modules:
  0.0 784.7 jit_solution(14308295725361192131)
XLA Ops:
  8.0 0.0 all-reduce.6.cloned.1.call-start
  8.1 0.8 slice_bitcast_fusion.1
  8.8 0.1 fusion.34
  8.9 17.6 %copy.22 = bf16[1,896,7168]{1,2,0:T(8,128)(2,1)} copy(bf16[1,896,7168]{2,1,0:T(8,128)(2,1)} %param.8) | data formatting | bytes 25690112 | tf_op args[1]
  26.5 17.5 %copy.25 = bf16[1,896,7168]{1,2,0:T(8,128)(2,1)} copy(bf16[1,896,7168]{2,1,0:T(8,128)(2,1)} %param.9) | data formatting | bytes 25690112 | tf_op args[2]
  44.0 1.2 sort.15
  45.4 12.8 %broadcast_select_fusion.1 = bf16[1,896,7168]{1,2,0:T(8,128)(2,1)} fusion(bf16[1,896,7168]{1,2,0:T(8,128)(2,1)} %copy.22, pred[]{:T(512)S(6)} %eq.56), kind=kLoop, calls=%fused_computation.22 | loop fusion | flops 6422528 | bytes 25690112 | tf_op jit(solution)/shard_map/jit(_where)/select_n | solution.py:8
  58.2 5.4 broadcast_select_fusion
  63.6 0.0 all-gather.3.cloned.1.call-start
  63.6 6.0 copy.27
  69.7 0.0 all-reduce.4.cloned.1.call-start
  69.7 0.1 select_reduce_fusion
  69.8 0.7 fusion.36
  71.2 436.6 %all-reduce.6.cloned.1.call-done = (bf16[1,896,7168]{1,2,0:T(8,128)(2,1)}, bf16[1,896,7168]{1,2,0:T(8,128)(2,1)}) async-done(((bf16[1,896,7168]{1,2,0:T(8,128)(2,1)}, bf16[1,896,7168]{1,2,0:T(8,128)(2,1)}), (bf16[1,896,7168]{1,2,0:T(8,128)(2,1)}, bf16[1,896,7168]{1,2,0:T(8,128)(2,1)})) %all-reduce.6.cloned.1.call-update) | async-done | bytes 25690128 | tf_op jit(solution)/shard_map/psum | solution.py:9
  507.8 16.3 %fusion.19 = bf16[512,7168]{0,1:T(8,128)(2,1)} fusion(bf16[1,896,7168]{1,2,0:T(8,128)(2,1)} %get-tuple-element.11, bf16[1,896,7168]{1,2,0:T(8,128)(2,1)} %copy.22, pred[]{:T(512)S(6)} %eq.55, bf16[1,512,896]{2,1,0:T(8,128)(2,1)S(1)} %copy-done), kind=kOutput, calls=%fused_computation.26 | convolution fusion | flops 6586761216 | bytes 33947648 | tf_op jit(solution)/shard_map/dot_general | solution.py:48
  524.1 0.6 fusion.37
  524.8 1.2 fusion.38
  526.0 173.0 %all-reduce.4.cloned.1.call-done = bf16[512,7168]{0,1:T(8,128)(2,1)} async-done(((bf16[512,7168]{0,1:T(8,128)(2,1)}), bf16[512,7168]{0,1:T(8,128)(2,1)}) %all-reduce.4.cloned.1.call-update) | async-done | bytes 7340048 | tf_op jit(solution)/shard_map/psum | solution.py:51
  699.0 27.9 %fusion.15 = bf16[1,896,7168]{1,2,0:T(8,128)(2,1)} fusion(bf16[1,896,7168]{1,2,0:T(8,128)(2,1)} %get-tuple-element.12, bf16[1,896,7168]{1,2,0:T(8,128)(2,1)} %copy.25, pred[]{:T(512)S(6)} %eq.55, f32[]{:T(128)} %fusion.38, bf16[1,512,7168]{1,2,0:T(8,128)(2,1)} %all-gather.3.cloned.1.call-done, bf16[512,7168]{0,1:T(8,128)(2,1)} %all-reduce.4.cloned.1.call-done, ...), kind=kOutput, calls=%fused_computation.24 | convolution fusion | flops 6715211776 | bytes 79822856 | tf_op jit(solution)/shard_map/dot_general | solution.py:56
  727.0 17.5 %copy.28 = bf16[1,896,7168]{2,1,0:T(8,128)(2,1)} copy(bf16[1,896,7168]{1,2,0:T(8,128)(2,1)} %fusion.15) | data formatting | bytes 25690112
  744.5 11.3 %add_multiply_fusion = f32[512,7168]{0,1:T(8,128)} fusion(bf16[512,7168]{0,1:T(8,128)(2,1)} %all-reduce.4.cloned.1.call-done), kind=kLoop, calls=%fused_computation.18 | loop fusion | flops 29360128 | bytes 22020096 | tf_op jit(solution)/shard_map/jvp()/mul | solution.py:13
  755.7 7.3 convert_element_type.34
  763.0 8.3 %fusion.23 = bf16[512,3584]{0,1:T(8,128)(2,1)} fusion(f32[512,7168]{0,1:T(8,128)} %add_multiply_fusion, s32[]{:T(128)S(6)} %select_n.63, f32[512,7168]{0,1:T(8,128)} %convert_element_type.34), kind=kLoop, calls=%fused_computation.28 | loop fusion | flops 3670016 | bytes 18350084 | tf_op jit(solution)/shard_map/convert_element_type | solution.py:19
  771.3 5.9 copy.24
  (25 shorter events, 0.1 us)
Async XLA Ops:
  8.0 499.8 %copy-start = (bf16[1,512,896]{2,1,0:T(8,128)(2,1)S(1)}, bf16[1,512,896]{2,1,0:T(8,128)(2,1)}, u32[]{:S(2)}) copy-start(bf16[1,512,896]{2,1,0:T(8,128)(2,1)} %param.7) | copy-start | bytes 2752516
  8.0 499.8 %all-reduce.6.cloned.1.call-start = ((), (), s32[]{:S(2)}) async-start(), calls=%async_computation.2 | async-start | bytes 51380224 | tf_op jit(solution)/shard_map/psum | solution.py:9
  44.0 14.1 %slice-start = ((s8[12845056]{0:T(1024)(128)(4,1)}), s8[262144]{0:T(1024)(128)(4,1)S(1)}, s32[]{:S(2)}) async-start(s8[12845056]{0:T(1024)(128)(4,1)} %bitcast.46), calls=%async_computation.3 | async-start | bytes 524288
  45.3 12.8 %slice-start.1 = ((s8[12845056]{0:T(1024)(128)(4,1)}), s8[4194304]{0:T(1024)(128)(4,1)S(1)}, s32[]{:S(2)}) async-start(s8[12845056]{0:T(1024)(128)(4,1)} %bitcast.46), calls=%async_computation.4 | async-start | bytes 8388608
  45.3 12.8 %slice-start.2 = ((s8[12845056]{0:T(1024)(128)(4,1)}), s8[4194304]{0:T(1024)(128)(4,1)S(1)}, s32[]{:S(2)}) async-start(s8[12845056]{0:T(1024)(128)(4,1)} %bitcast.46), calls=%async_computation.5 | async-start | bytes 8388608
  45.3 12.8 %slice-start.3 = ((s8[12845056]{0:T(1024)(128)(4,1)}), s8[4194304]{0:T(1024)(128)(4,1)S(1)}, s32[]{:S(2)}) async-start(s8[12845056]{0:T(1024)(128)(4,1)} %bitcast.46), calls=%async_computation.6 | async-start | bytes 8388608
  63.6 462.4 %all-gather.3.cloned.1.call-start = ((), (), s32[]{:S(2)}) async-start(), calls=%async_computation.1 | async-start | bytes 11010048 | tf_op jit(solution)/shard_map/all_gather | solution.py:50
  69.7 629.3 %all-reduce.4.cloned.1.call-start = ((), (), s32[]{:S(2)}) async-start(), calls=%async_computation | async-start | bytes 14680064 | tf_op jit(solution)/shard_map/psum | solution.py:51
  507.8 16.3 %copy-start.3 = (s32[16]{0:T(128)S(1)}, s32[16]{0:T(128)}, u32[]{:S(2)}) copy-start(s32[16]{0:T(128)} %param.12) | copy-start | bytes 196
  507.8 17.0 %copy-start.4 = (f32[8]{0:T(128)S(1)}, f32[8]{0:T(128)}, u32[]{:S(2)}) copy-start(f32[8]{0:T(128)} %param.13) | copy-start | bytes 100
  744.5 11.3 %copy-start.2 = (bf16[512,7168]{0,1:T(8,128)(2,1)S(1)}, bf16[512,7168]{0,1:T(8,128)(2,1)}, u32[]{:S(2)}) copy-start(bf16[512,7168]{0,1:T(8,128)(2,1)} %all-reduce.4.cloned.1.call-done) | copy-start | bytes 22020100
  755.7 21.5 %copy-start.1 = (bf16[1,512,896]{2,1,0:T(8,128)(2,1)S(1)}, bf16[1,512,896]{2,1,0:T(8,128)(2,1)}, u32[]{:S(2)}) copy-start(bf16[1,512,896]{2,1,0:T(8,128)(2,1)} %param.7) | copy-start | bytes 2752516
Sparse Core Ops, SparseCore 0:
  63.7 444.0 all-reduce.5
Sparse Core Ops, SparseCore 1:
  69.8 90.0 all-gather.2
  524.2 174.8 all-reduce.3
where the time goes:
time: 788 us; the launch traced here: 785 us
  waiting for transfers between devices  610 us (77%)
  local copies, waits for them, and re-layouts  65.3 us (8%)
  other arithmetic  49 us (6%)
  matrix products  44.2 us (6%)
  between operations  16.3 us (2%)
    psum x1, waiting for transfers between devices, from_root(): return lax.psum(kept, axis)  437 us
    psum x1, waiting for transfers between devices, local(): lax.psum(partial_value.astype(jnp.bfloat16), 'tp').astype(jnp.float32)  173 us
    unnamed x22, local copies, waits for them, and re-layouts  58.6 us
    dot_general x1, matrix products, local(): lax.dot_general(inputs, grad_hidden, (((0,), (0,)), ((), ())), preferred_...  27.9 us
    select_n x2, other arithmetic, from_root(): jnp.where(lax.axis_index(axis) == source, value, 0).astype(value.dtype)  18.2 us
    dot_general x1, matrix products, local(): jnp.dot(inputs, taken_weight, preferred_element_type=jnp.float32)  16.3 us
  transfers between devices with their start and end apart: 3, of which 2 were waited for; matrix products, arithmetic and copies ran while one was open for 3% of the time, Pallas kernels for 0%

commit v1 on v0

v1 whole, which is shorter than its diff:
```python
import functools

import jax
import jax.numpy as jnp
from jax import lax
from jax.experimental import pallas as pl
from jax.experimental.pallas import tpu as pltpu
from jax.sharding import PartitionSpec as P

MESH = pl.DeviceIdType.MESH
ROWS = 16
PIECES = 2


def ring_of(member, members):
    core = member % 2
    y = (member // 2) % 2
    z = member // 4
    half = members // 4
    chip = z * (1 - y) + (2 * half - 1 - z) * y
    return 2 * chip + core


def member_at(place, members):
    core = place % 2
    chip = place // 2
    half = members // 4
    y = chip // half
    z = chip * (1 - y) + (2 * half - 1 - chip) * y
    return (2 * z + y) * 2 + core


def gelu_tanh(value):
    return jax.nn.gelu(value, approximate=True)


def activate(hidden, cot_block):
    active, pullback = jax.vjp(gelu_tanh, hidden)
    grad_hidden = pullback(cot_block.astype(jnp.float32))[0].astype(jnp.bfloat16)
    return (active.astype(jnp.bfloat16), grad_hidden)


def spread_kernel(members, table, own, out, came, sent, send_sem, recv_sem):
    rows, cols = own.shape
    blocks = rows // 2 // ROWS
    steps = blocks + members - 2
    width = cols // PIECES
    place = ring_of(lax.axis_index("pop"), members)
    ahead = member_at((place + 1) % members, members)
    behind = member_at((place + members - 1) % members, members)
    is_root = table[0] > 0
    chosen = table[1] > 0
    targets = (ahead, behind)

    barrier = pltpu.get_barrier_semaphore()
    for near in targets:
        pl.semaphore_signal(barrier, inc=1, device_id={"pop": near}, device_id_type=MESH)
    pl.semaphore_wait(barrier, 2)

    def copy_of(way, step, piece):
        slot = step % 2
        cut = pl.ds(piece * width, width)
        return pltpu.make_async_remote_copy(
            src_ref=sent.at[way, slot, :, cut],
            dst_ref=came.at[way, step, :, cut],
            send_sem=send_sem.at[way, slot, piece],
            recv_sem=recv_sem.at[way, step, piece],
            device_id={"pop": targets[way]},
            device_id_type=MESH,
        )

    def own_rows(way, step):
        first = way * (rows // 2) + jnp.minimum(step, blocks - 1) * ROWS
        return pl.ds(pl.multiple_of(first, ROWS), ROWS)

    for piece in range(PIECES):
        cut = pl.ds(piece * width, width)
        for way in range(2):
            sent[way, 0, :, cut] = own[way * (rows // 2) : way * (rows // 2) + ROWS, cut]
            copy_of(way, 0, piece).start()

    def forward(step, carry):
        for piece in range(PIECES):
            cut = pl.ds(piece * width, width)
            for way in range(2):
                copy_of(way, step - 1, piece).wait_recv()

                @pl.when(step >= 2)
                def _():
                    copy_of(way, step - 2, piece).wait_send()

                sent[way, step % 2, :, cut] = jnp.where(
                    is_root, own[own_rows(way, step), cut], came[way, step - 1, :, cut]
                )
                copy_of(way, step, piece).start()
        return carry

    lax.fori_loop(1, steps, forward, 0)
    for piece in range(PIECES):
        for way in range(2):
            copy_of(way, steps - 1, piece).wait_recv()
            copy_of(way, steps - 2, piece).wait_send()
            copy_of(way, steps - 1, piece).wait_send()

    def settle(block, carry):
        for way in range(2):
            at = pl.ds(pl.multiple_of(way * (rows // 2) + block * ROWS, ROWS), ROWS)
            out[at, :] = jnp.where(chosen, came[way, block + table[2 + way]], own[at, :])
        return carry

    lax.fori_loop(0, blocks, settle, 0)


def spread(value, table, members, turn):
    rows, cols = value.shape
    steps = rows // 2 // ROWS + members - 2
    return pl.pallas_call(
        functools.partial(spread_kernel, members),
        out_shape=jax.ShapeDtypeStruct(value.shape, value.dtype),
        in_specs=[
            pl.BlockSpec(memory_space=pltpu.SMEM),
            pl.BlockSpec(memory_space=pltpu.VMEM),
        ],
        out_specs=pl.BlockSpec(memory_space=pltpu.VMEM),
        scratch_shapes=[
            pltpu.VMEM((2, steps, ROWS, cols), value.dtype),
            pltpu.VMEM((2, 2, ROWS, cols), value.dtype),
            pltpu.SemaphoreType.DMA((2, 2, PIECES)),
            pltpu.SemaphoreType.DMA((2, steps, PIECES)),
        ],
        compiler_params=pltpu.CompilerParams(
            collective_id=turn, has_side_effects=True, vmem_limit_bytes=60 * 2**20
        ),
        cost_estimate=pl.CostEstimate(
            flops=0, bytes_accessed=300 * 2**20, transcendentals=0
        ),
        name=f"spread_{turn}",
    )(table, value)


def local(tokens, weight, momentum, cotangent, assignment, lr_index, rates):
    members = lax.axis_size("pop")
    ranks = lax.axis_size("tp")
    me = lax.axis_index("pop")
    side = lax.axis_index("tp")
    member_ids = jnp.arange(members, dtype=jnp.int32)
    hit = assignment[:, 0] == me
    my_source = jnp.where(jnp.any(hit), jnp.sum(jnp.where(hit, assignment[:, 1], 0)), me)
    my_index = jnp.sum(jnp.where(member_ids == me, lr_index, 0))
    rate_ids = jnp.arange(rates.shape[0], dtype=jnp.int32)
    my_rate = jnp.sum(jnp.where(rate_ids == my_index, rates, 0.0))
    tops = assignment.shape[0] // 4
    winner_hit = assignment[:, 1][None, :] == member_ids[:, None]
    present = jnp.any(winner_hit, axis=1)
    roots = jnp.sort(jnp.where(present, member_ids, members))[:tops]
    place = ring_of(me, members)
    tables = []
    for turn in range(tops):
        root = roots[turn]
        behind = (place - ring_of(root, members) + members) % members
        before = (members - behind) % members
        tables.append(
            jnp.stack(
                [
                    (me == root).astype(jnp.int32),
                    jnp.logical_and(my_source == root, me != root).astype(jnp.int32),
                    jnp.maximum(behind - 1, 0).astype(jnp.int32),
                    jnp.maximum(before - 1, 0).astype(jnp.int32),
                ]
            )
        )

    def take(value, first):
        taken = value
        for turn in range(tops):
            arrived = spread(value if turn == 0 else value + 0, tables[turn], members, first + turn)
            taken = arrived if turn == 0 else jnp.where(my_source == roots[turn], arrived, taken)
        return taken

    inputs = tokens[0]
    share_cols = cotangent.shape[2]
    taken_weight = take(weight[0], 0)
    partial_value = jnp.dot(inputs, taken_weight, preferred_element_type=jnp.float32)
    partial_value = partial_value.astype(jnp.bfloat16)
    if ranks == 2:
        swap = [(0, 1), (1, 0)]
        left, right = partial_value[:, :share_cols], partial_value[:, share_cols:]
        mine = jnp.where(side == 0, left, right)
        theirs = jnp.where(side == 0, right, left)
        theirs, raw_momentum = lax.optimization_barrier((theirs, momentum[0]))
        arrived = lax.ppermute(theirs, "tp", swap)
        taken_momentum = take(raw_momentum, tops)
        hidden = mine.astype(jnp.float32) + arrived.astype(jnp.float32)
        active, grad_mine = activate(hidden, cotangent[0])
        grad_theirs = lax.ppermute(grad_mine, "tp", swap)
        grad_hidden = jnp.concatenate(
            [
                jnp.where(side == 0, grad_mine, grad_theirs),
                jnp.where(side == 0, grad_theirs, grad_mine),
            ],
            axis=1,
        )
    else:
        taken_momentum = take(momentum[0], tops)
        hidden = lax.psum_scatter(
            partial_value, "tp", scatter_dimension=1, tiled=True
        ).astype(jnp.float32)
        active, grad_mine = activate(hidden, cotangent[0])
        grad_hidden = lax.all_gather(grad_mine, "tp", axis=1, tiled=True)
    grad_weight = lax.dot_general(
        inputs, grad_hidden, (((0,), (0,)), ((), ())), preferred_element_type=jnp.float32
    )
    new_momentum = 0.9 * taken_momentum.astype(jnp.float32) + grad_weight
    updated = (taken_weight.astype(jnp.float32) - my_rate * new_momentum).astype(jnp.bfloat16)
    return (active[None], updated[None])


def solution(mesh):
    placed = (
        P("pop", None, "tp"),
        P("pop", "tp", None),
        P("pop", "tp", None),
        P("pop", None, "tp"),
        P(),
        P(),
        P(),
    )
    return jax.shard_map(
        local,
        mesh=mesh,
        in_specs=placed,
        out_specs=(P("pop", None, "tp"), P("pop", "tp", None)),
        check_vma=False,
    )
```

time: 788 us -> 428 us (0.54)
  waiting for transfers between devices: 610 us -> 73.5 us
  Pallas kernels: 0 us -> 271 us
  local copies, waits for them, and re-layouts: 65.3 us -> 15.6 us
  other arithmetic: 49 us -> 27.2 us
  between operations: 16.3 us -> 2.36 us
  matrix products: 44.2 us -> 35 us
    psum x2 -> x0, waiting for transfers between devices: 610 us -> none  [the longest x1 437 us: from_root(): return lax.psum(kept, axis)]
    pallas_call x0 -> x2, Pallas kernels: none -> 271 us  [spread(): pl.pallas_call(functools.partial(spread_kernel, members), out_shape=jax.S...]
    ppermute x0 -> x2, waiting for transfers between devices: none -> 73.5 us  [the longest x1 73.5 us: local(): arrived = lax.ppermute(theirs, 'tp', swap)]
    unnamed x22 -> x10, local copies, waits for them, and re-layouts: 58.6 us -> 14.9 us
    mul x1 -> x0, other arithmetic: 11.3 us -> none  [gelu_tanh(): return jax.nn.gelu(value, approximate=True)]
    select_n x2, other arithmetic: 18.2 us -> 8.77 us  [the longest x1 6.56 us: local(): jnp.where(side == 0, grad_mine, grad_theirs)]
  transfers between devices with their start and end apart: 3 -> 2, of which waited for: 2 -> 1; matrix products, arithmetic and copies ran while one was open for 3% -> 3% of each run, Pallas kernels for 0% -> 32%
where the time goes in v1:
time: 428 us; the launch traced here: 427 us
  Pallas kernels  271 us (63%)
  waiting for transfers between devices  73.5 us (17%)
  matrix products  35 us (8%)
  other arithmetic  27.2 us (6%)
  local copies, waits for them, and re-layouts  15.6 us (4%)
    pallas_call x2, Pallas kernels, spread(): pl.pallas_call(functools.partial(spread_kernel, members), out_shape=jax.S...  271 us
    ppermute x1, waiting for transfers between devices, local(): arrived = lax.ppermute(theirs, 'tp', swap)  73.5 us
    dot_general x1, matrix products, local(): lax.dot_general(inputs, grad_hidden, (((0,), (0,)), ((), ())), preferred_...  22.2 us
    unnamed x10, local copies, waits for them, and re-layouts  14.9 us
    dot_general x1, matrix products, local(): jnp.dot(inputs, taken_weight, preferred_element_type=jnp.float32)  12.8 us
    convert_element_type x1, other arithmetic, activate(): pullback(cot_block.astype(jnp.float32))[0].astype(jnp.bfloat16)  11.7 us
  transfers between devices with their start and end apart: 2, of which 1 were waited for; matrix products, arithmetic and copies ran while one was open for 3% of the time, Pallas kernels for 32%

profile of v1, /device:TPU:1, one launch (start us, length us, event | category | flops | bytes accessed | tf_op | source)
XLA Modules:
  0.0 427.4 jit_solution(1098135487105302523)
XLA Ops:
  0.6 0.0 copy-start
  0.7 1.4 fusion.24
  2.1 1.4 compare_reduce_fusion
  3.5 0.7 slice_bitcast_fusion
  4.2 0.1 fusion.21
  4.3 1.2 sort.15
  7.1 0.6 pad_add_fusion.table
  7.8 135.8 %spread_0.1 = bf16[896,7168]{1,0:T(8,128)(2,1)} custom-call(s32[4]{0:T(128)} %pad_add_fusion.table, bf16[896,7168]{1,0:T(8,128)(2,1)} %bitcast.41), custom_call_target="tpu_custom_call" | custom-call | bytes 314572800 | tf_op jit(solution)/shard_map/spread_0/pallas_call | solution.py:117
  143.5 12.8 %fusion.4 = bf16[512,7168]{0,1:T(8,128)(2,1)S(1)} fusion(bf16[896,7168]{1,0:T(8,128)(2,1)} %spread_0.1, bf16[1,512,896]{2,1,0:T(8,128)(2,1)S(1)} %copy-done), kind=kOutput, calls=%fused_computation.8 | convolution fusion | flops 6580338688 | bytes 21102592 | tf_op jit(solution)/shard_map/dot_general | solution.py:183
  156.3 0.0 copy-start.1
  156.3 3.0 copy-done.1
  159.4 2.2 broadcast_select_fusion.2
  161.6 1.2 collective-permute-start
  162.8 6.0 %copy.12 = bf16[1,512,3584]{1,2,0:T(8,128)(2,1)} copy(bf16[1,512,3584]{2,1,0:T(8,128)(2,1)} %param.10) | data formatting | bytes 7340032 | tf_op args[3]
  168.8 73.5 %collective-permute-done = bf16[512,3584]{0,1:T(8,128)(2,1)} collective-permute-done((bf16[512,3584]{0,1:T(8,128)(2,1)}, bf16[512,3584]{0,1:T(8,128)(2,1)}, u32[]{:S(2)}, u32[]{:S(2)}) %collective-permute-start) | collective-permute-done | bytes 3670048 | tf_op jit(solution)/shard_map/ppermute | solution.py:191
  242.3 11.7 %fusion.7 = (bf16[512,3584]{0,1:T(8,128)(2,1)}, bf16[1,512,3584]{1,2,0:T(8,128)(2,1)}) fusion(bf16[512,3584]{0,1:T(8,128)(2,1)} %collective-permute-done, bf16[1,512,3584]{1,2,0:T(8,128)(2,1)} %copy.12, bf16[512,7168]{0,1:T(8,128)(2,1)} %copy-done.1, pred[]{:T(512)S(6)} %eq.55), kind=kLoop, calls=%fused_computation.13 | loop fusion | flops 49545216 | bytes 22020096 | tf_op jit(solution)/shard_map/convert_element_type | solution.py:39
  254.0 1.3 collective-permute-start.1
  255.3 135.5 %spread_1.1 = bf16[896,7168]{1,0:T(8,128)(2,1)} custom-call(s32[4]{0:T(128)} %pad_add_fusion.table, bf16[896,7168]{1,0:T(8,128)(2,1)} %bitcast.42), custom_call_target="tpu_custom_call" | custom-call | bytes 314572800 | tf_op jit(solution)/shard_map/spread_1/pallas_call | solution.py:117
  390.8 0.6 fusion.22
  391.4 1.3 fusion.23
  392.7 5.9 %copy.14 = bf16[1,512,3584]{2,1,0:T(8,128)(2,1)} copy(bf16[1,512,3584]{1,2,0:T(8,128)(2,1)} %get-tuple-element.14) | data formatting | bytes 7340032
  398.6 0.0 collective-permute-done.1
  398.6 6.6 %broadcast_select_fusion.1 = (bf16[512,3584]{0,1:T(8,128)(2,1)}, bf16[512,3584]{0,1:T(8,128)(2,1)}) fusion(bf16[512,3584]{0,1:T(8,128)(2,1)} %get-tuple-element.13, bf16[512,3584]{0,1:T(8,128)(2,1)} %collective-permute-done.1, pred[]{:T(512)S(6)} %eq.55), kind=kLoop, calls=%fused_computation.28 | loop fusion | flops 3670016 | bytes 14680065 | tf_op jit(solution)/shard_map/jit(_where)/select_n | solution.py:198
  405.2 22.2 %fusion.3 = bf16[1,896,7168]{2,1,0:T(8,128)(2,1)} fusion(bf16[896,7168]{1,0:T(8,128)(2,1)} %spread_1.1, f32[]{:T(128)} %fusion.23, bf16[896,7168]{1,0:T(8,128)(2,1)} %spread_0.1, bf16[512,3584]{0,1:T(8,128)(2,1)} %get-tuple-element.16, bf16[512,3584]{0,1:T(8,128)(2,1)} %get-tuple-element.15, bf16[1,512,896]{2,1,0:T(8,128)(2,1)S(1)} %copy-done), kind=kOutput, calls=%fused_computation.4 | convolution fusion | flops 6636306432 | bytes 46792708 | tf_op jit(solution)/shard_map/dot_general | solution.py:210
  (7 shorter events, 0.0 us)
Async XLA Ops:
  0.6 142.9 %copy-start = (bf16[1,512,896]{2,1,0:T(8,128)(2,1)S(1)}, bf16[1,512,896]{2,1,0:T(8,128)(2,1)}, u32[]{:S(2)}) copy-start(bf16[1,512,896]{2,1,0:T(8,128)(2,1)} %param.7) | copy-start | bytes 2752516
  156.3 3.1 copy-start.1
  161.6 80.7 %collective-permute-start = (bf16[512,3584]{0,1:T(8,128)(2,1)}, bf16[512,3584]{0,1:T(8,128)(2,1)}, u32[]{:S(2)}, u32[]{:S(2)}) collective-permute-start(bf16[512,3584]{0,1:T(8,128)(2,1)} %broadcast_select_fusion.2), channel_id=1, source_target_pairs={{0,1},{1,0},{2,3},{3,2},{4,5},{5,4},{6,7},{7,6},{8,9},{9,8},{10,11... | collective-permute-start | bytes 11010056 | tf_op jit(solution)/shard_map/ppermute | solution.py:191
  254.0 136.8 %copy-start.2 = (s32[16]{0:T(128)S(1)}, s32[16]{0:T(128)}, u32[]{:S(2)}) copy-start(s32[16]{0:T(128)} %param.12) | copy-start | bytes 196
  254.0 137.4 %copy-start.3 = (f32[8]{0:T(128)S(1)}, f32[8]{0:T(128)}, u32[]{:S(2)}) copy-start(f32[8]{0:T(128)} %param.13) | copy-start | bytes 100
  254.0 144.6 %collective-permute-start.1 = (bf16[512,3584]{0,1:T(8,128)(2,1)}, bf16[512,3584]{0,1:T(8,128)(2,1)}, u32[]{:S(2)}, u32[]{:S(2)}) collective-permute-start(bf16[512,3584]{0,1:T(8,128)(2,1)} %get-tuple-element.13), channel_id=1, source_target_pairs={{0,1},{1,0},{2,3},{3,2},{4,5},{5,4},{6,7},{7,6},{8,9},{9,8},{10,11... | collective-permute-start | bytes 11010056 | tf_op jit(solution)/shard_map/ppermute | solution.py:195

commit v2 on v1

--- a/solution.py
+++ b/solution.py
@@ -8,8 +8,8 @@
 from jax.sharding import PartitionSpec as P
 
 MESH = pl.DeviceIdType.MESH
-ROWS = 16
-PIECES = 2
+PIECES = 4
+TILE = 512
 
 
 def ring_of(member, members):
@@ -40,7 +40,12 @@
     return (active.astype(jnp.bfloat16), grad_hidden)
 
 
-def spread_kernel(members, table, own, out, came, sent, send_sem, recv_sem):
+def rows_of(rows, cols, whole_cols):
+    wanted = 16 * (whole_cols // cols)
+    return wanted if (rows // 2) % wanted == 0 else 16
+
+
+def spread_kernel(members, ROWS, table, own, out, came, sent, send_sem, recv_sem):
     rows, cols = own.shape
     blocks = rows // 2 // ROWS
     steps = blocks + members - 2
@@ -111,20 +116,23 @@
     lax.fori_loop(0, blocks, settle, 0)
 
 
-def spread(value, table, members, turn):
-    rows, cols = value.shape
-    steps = rows // 2 // ROWS + members - 2
+def spread(value, table, members, turn, part, parts):
+    rows, whole_cols = value.shape
+    cols = whole_cols // parts
+    height = rows_of(rows, cols, whole_cols)
+    steps = rows // 2 // height + members - 2
     return pl.pallas_call(
-        functools.partial(spread_kernel, members),
-        out_shape=jax.ShapeDtypeStruct(value.shape, value.dtype),
+        functools.partial(spread_kernel, members, height),
+        grid=(1,),
+        out_shape=jax.ShapeDtypeStruct((rows, cols), value.dtype),
         in_specs=[
             pl.BlockSpec(memory_space=pltpu.SMEM),
-            pl.BlockSpec(memory_space=pltpu.VMEM),
+            pl.BlockSpec((rows, cols), lambda i: (0, part), pipeline_mode=pl.Buffered(1)),
         ],
-        out_specs=pl.BlockSpec(memory_space=pltpu.VMEM),
+        out_specs=pl.BlockSpec((rows, cols), lambda i: (0, 0), pipeline_mode=pl.Buffered(1)),
         scratch_shapes=[
-            pltpu.VMEM((2, steps, ROWS, cols), value.dtype),
-            pltpu.VMEM((2, 2, ROWS, cols), value.dtype),
+            pltpu.VMEM((2, steps, height, cols), value.dtype),
+            pltpu.VMEM((2, 2, height, cols), value.dtype),
             pltpu.SemaphoreType.DMA((2, 2, PIECES)),
             pltpu.SemaphoreType.DMA((2, steps, PIECES)),
         ],
@@ -132,10 +140,52 @@
             collective_id=turn, has_side_effects=True, vmem_limit_bytes=60 * 2**20
         ),
         cost_estimate=pl.CostEstimate(
-            flops=0, bytes_accessed=300 * 2**20, transcendentals=0
+            flops=0, bytes_accessed=300 * 2**20 // parts, transcendentals=0
         ),
         name=f"spread_{turn}",
     )(table, value)
+
+
+def update_kernel(half, side, rate, turned, mine, theirs, weight, first, second, out):
+    block = pl.program_id(0)
+    grad = jnp.where(block // half == side[0], mine[...], theirs[...])
+    grad_weight = jnp.dot(turned[...], grad, preferred_element_type=jnp.float32)
+    momentum = jnp.where(block < half, first[...], second[...]).astype(jnp.float32)
+    new_momentum = 0.9 * momentum + grad_weight
+    out[...] = (weight[...].astype(jnp.float32) - rate[0] * new_momentum).astype(out.dtype)
+
+
+def update(side, rate, turned, mine, theirs, weight, first, second):
+    rows, cols = weight.shape
+    tokens = turned.shape[1]
+    half = cols // 2 // TILE
+    near = lambda j, side: (0, jnp.clip(j - side[0] * half, 0, half - 1))
+    far = lambda j, side: (0, jnp.clip(j - (1 - side[0]) * half, 0, half - 1))
+    return pl.pallas_call(
+        functools.partial(update_kernel, half),
+        grid_spec=pltpu.PrefetchScalarGridSpec(
+            num_scalar_prefetch=1,
+            grid=(2 * half,),
+            in_specs=[
+                pl.BlockSpec(memory_space=pltpu.SMEM),
+                pl.BlockSpec((rows, tokens), lambda j, side: (0, 0)),
+                pl.BlockSpec((tokens, TILE), near),
+                pl.BlockSpec((tokens, TILE), far),
+                pl.BlockSpec((rows, TILE), lambda j, side: (0, j)),
+                pl.BlockSpec((rows, TILE), lambda j, side: (0, jnp.minimum(j, half - 1))),
+                pl.BlockSpec((rows, TILE), lambda j, side: (0, jnp.maximum(j - half, 0))),
+            ],
+            out_specs=pl.BlockSpec((rows, TILE), lambda j, side: (0, j)),
+        ),
+        out_shape=jax.ShapeDtypeStruct(weight.shape, weight.dtype),
+        compiler_params=pltpu.CompilerParams(vmem_limit_bytes=40 * 2**20),
+        cost_estimate=pl.CostEstimate(
+            flops=2 * rows * cols * tokens,
+            bytes_accessed=6 * rows * cols,
+            transcendentals=0,
+        ),
+        name="update",
+    )(side, rate, turned, mine, theirs, weight, first, second)
 
 
 def local(tokens, weight, momentum, cotangent, assignment, lr_index, rates):
@@ -170,11 +220,14 @@
             )
         )
 
-    def take(value, first):
-        taken = value
+    def take(value, first, part=0, parts=1):
+        taken = None
         for turn in range(tops):
-            arrived = spread(value if turn == 0 else value + 0, tables[turn], members, first + turn)
-            taken = arrived if turn == 0 else jnp.where(my_source == roots[turn], arrived, taken)
+            arrived = spread(value, tables[turn], members, first + turn, part, parts)
+            if taken is None:
+                taken = arrived
+            else:
+                taken = jnp.where(my_source == roots[turn], arrived, taken)
         return taken
 
     inputs = tokens[0]
@@ -189,16 +242,22 @@
         theirs = jnp.where(side == 0, right, left)
         theirs, raw_momentum = lax.optimization_barrier((theirs, momentum[0]))
         arrived = lax.ppermute(theirs, "tp", swap)
-        taken_momentum = take(raw_momentum, tops)
+        first = take(raw_momentum, tops, 0, 2)
+        arrived, first = lax.optimization_barrier((arrived, first))
         hidden = mine.astype(jnp.float32) + arrived.astype(jnp.float32)
         active, grad_mine = activate(hidden, cotangent[0])
+        grad_mine, raw_momentum = lax.optimization_barrier((grad_mine, raw_momentum))
         grad_theirs = lax.ppermute(grad_mine, "tp", swap)
-        grad_hidden = jnp.concatenate(
-            [
-                jnp.where(side == 0, grad_mine, grad_theirs),
-                jnp.where(side == 0, grad_theirs, grad_mine),
-            ],
-            axis=1,
+        second = take(raw_momentum, 2 * tops, 1, 2)
+        updated = update(
+            side.astype(jnp.int32).reshape(1),
+            my_rate.reshape(1),
+            inputs.T,
+            grad_mine,
+            grad_theirs,
+            taken_weight,
+            first,
+            second,
         )
     else:
         taken_momentum = take(momentum[0], tops)
@@ -207,11 +266,12 @@
         ).astype(jnp.float32)
         active, grad_mine = activate(hidden, cotangent[0])
         grad_hidden = lax.all_gather(grad_mine, "tp", axis=1, tiled=True)
-    grad_weight = lax.dot_general(
-        inputs, grad_hidden, (((0,), (0,)), ((), ())), preferred_element_type=jnp.float32
-    )
-    new_momentum = 0.9 * taken_momentum.astype(jnp.float32) + grad_weight
-    updated = (taken_weight.astype(jnp.float32) - my_rate * new_momentum).astype(jnp.bfloat16)
+        grad_weight = lax.dot_general(
+            inputs, grad_hidden, (((0,), (0,)), ((), ())), preferred_element_type=jnp.float32
+        )
+        new_momentum = 0.9 * taken_momentum.astype(jnp.float32) + grad_weight
+        updated = taken_weight.astype(jnp.float32) - my_rate * new_momentum
+        updated = updated.astype(jnp.bfloat16)
     return (active[None], updated[None])
 
 

time: 428 us -> 363 us (0.85)
  waiting for transfers between devices: 73.5 us -> 0.01 us
  Pallas kernels: 271 us -> 321 us
  matrix products: 35 us -> 12.6 us
  local copies, waits for them, and re-layouts: 15.6 us -> 5.2 us
  other arithmetic: 27.2 us -> 19.9 us
    ppermute x1, waiting for transfers between devices: 73.5 us -> 0.01 us  [local(): arrived = lax.ppermute(theirs, 'tp', swap)]
    pallas_call x2 -> x4, Pallas kernels: 271 us -> 321 us  [the longest x3 297 us: spread(): pl.pallas_call(functools.partial(spread_kernel, members, height), grid=(1...]
    dot_general x1 -> x0, matrix products: 22.2 us -> none  [local(): lax.dot_general(inputs, grad_hidden, (((0,), (0,)), ((), ())), preferred_...]
    unnamed x10 -> x11, local copies, waits for them, and re-layouts: 14.9 us -> 4.51 us
    select_n x1 -> x0, other arithmetic: 6.56 us -> none  [local(): jnp.where(side == 0, grad_mine, grad_theirs)]
  transfers between devices with their start and end apart: 2 -> 2, of which waited for: 1 -> 0; matrix products, arithmetic and copies ran while one was open for 3% -> 1% of each run, Pallas kernels for 32% -> 47%
where the time goes in v2:
time: 363 us
  Pallas kernels  321 us (88%)
  other arithmetic  19.9 us (5%)
  matrix products  12.6 us (3%)
  local copies, waits for them, and re-layouts  5.2 us (1%)
    pallas_call x3, Pallas kernels, spread(): pl.pallas_call(functools.partial(spread_kernel, members, height), grid=(1...  297 us
    pallas_call x1, Pallas kernels, update(): pl.pallas_call(functools.partial(update_kernel, half), grid_spec=pltpu.Pr...  23.8 us
    dot_general x1, matrix products, local(): jnp.dot(inputs, taken_weight, preferred_element_type=jnp.float32)  12.6 us
    convert_element_type x1, other arithmetic, activate(): pullback(cot_block.astype(jnp.float32))[0].astype(jnp.bfloat16)  11.1 us
  transfers between devices with their start and end apart: 2, of which 0 were waited for; matrix products, arithmetic and copies ran while one was open for 1% of the time, Pallas kernels for 47%

profile of v2, /device:TPU:1, one launch (start us, length us, event | category | flops | bytes accessed | tf_op | source)
XLA Modules:
  0.0 362.5 jit_solution(4514237452570567152)
XLA Ops:
  0.7 1.4 fusion.16
  2.0 1.4 compare_reduce_fusion
  3.4 0.7 slice_bitcast_fusion
  4.1 0.1 fusion.13
  4.2 1.2 sort.15
  7.1 0.6 pad_add_fusion.table
  7.7 127.1 %spread_0.1.weight = bf16[896,7168]{1,0:T(8,128)(2,1)} custom-call(s32[4]{0:T(128)} %pad_add_fusion.table, bf16[896,7168]{1,0:T(8,128)(2,1)} %bitcast.36), custom_call_target="tpu_custom_call" | custom-call | bytes 314572800 | tf_op jit(solution)/shard_map/spread_0/pallas_call | solution.py:124
  134.8 12.6 %fusion = bf16[512,7168]{1,0:T(8,128)(2,1)S(1)} fusion(bf16[896,7168]{1,0:T(8,128)(2,1)} %spread_0.1.weight, bf16[1,512,896]{2,1,0:T(8,128)(2,1)S(1)} %copy-done.2), kind=kOutput, calls=%fused_computation.3 | convolution fusion | flops 6580338688 | bytes 21102592 | tf_op jit(solution)/shard_map/dot_general | solution.py:236
  147.4 0.0 copy-start
  147.4 3.0 copy-done
  150.5 2.2 broadcast_select_fusion
  152.7 1.2 collective-permute-start
  153.9 85.1 %spread_1.1.first = bf16[896,3584]{1,0:T(8,128)(2,1)} custom-call(s32[4]{0:T(128)} %pad_add_fusion.table, bf16[896,7168]{1,0:T(8,128)(2,1)} %bitcast.34), custom_call_target="tpu_custom_call" | custom-call | bytes 157286400 | tf_op jit(solution)/shard_map/spread_1/pallas_call | solution.py:124
  238.9 0.0 copy-start.3
  239.0 0.0 copy-start.4
  239.0 0.0 collective-permute-done
  239.0 11.1 %fusion.3 = (bf16[512,3584]{1,0:T(8,128)(2,1)}, bf16[1,512,3584]{2,1,0:T(8,128)(2,1)}) fusion(bf16[512,3584]{1,0:T(8,128)(2,1)} %collective-permute-done, bf16[1,512,3584]{2,1,0:T(8,128)(2,1)S(1)} %copy-done.1, bf16[512,7168]{1,0:T(8,128)(2,1)} %copy-done, pred[]{:T(512)S(6)} %eq.53), kind=kLoop, calls=%fused_computation.8 | loop fusion | flops 49545216 | bytes 22020096 | tf_op jit(solution)/shard_map/convert_element_type | solution.py:39
  250.1 0.5 collective-permute-start.1
  250.6 1.5 copy.11
  252.1 0.6 fusion.14
  252.7 1.2 fusion.15
  253.9 84.7 %spread_2.1.second = bf16[896,3584]{1,0:T(8,128)(2,1)} custom-call(s32[4]{0:T(128)} %pad_add_fusion.table, bf16[896,7168]{1,0:T(8,128)(2,1)} %bitcast.35), custom_call_target="tpu_custom_call" | custom-call | bytes 157286400 | tf_op jit(solution)/shard_map/spread_2/pallas_call | solution.py:124
  338.7 0.0 collective-permute-done.1.theirs
  338.7 23.8 %update.1 = bf16[896,7168]{1,0:T(8,128)(2,1)} custom-call(s32[1]{0:T(128)} %bitcast.12.side, f32[1]{0:T(128)} %bitcast.13.rate, bf16[896,512]{1,0:T(8,128)(2,1)S(1)} %bitcast.33, bf16[512,3584]{1,0:T(8,128)(2,1)} %get-tuple-element.14.mine, bf16[512,3584]{1,0:T(8,128)(2,1)} %collective-permute-done.1.theirs, bf16[896,7168]{1,0:T(8,128)(2,1)} %spread_0.1.weight, ...), custom_call_target="tpu_custom_call" | custom-call | flops 6576668672 | bytes 38535168 | tf_op jit(solution)/shard_map/update/pallas_call | solution.py:164
  (8 shorter events, 0.0 us)
Async XLA Ops:
  7.7 127.1 %copy-start.2 = (bf16[1,512,896]{2,1,0:T(8,128)(2,1)S(1)}, bf16[1,512,896]{2,1,0:T(8,128)(2,1)}, u32[]{:S(2)}) copy-start(bf16[1,512,896]{2,1,0:T(8,128)(2,1)} %param.7) | copy-start | bytes 2752516
  147.4 3.1 copy-start
  152.7 86.3 %copy-start.1 = (bf16[1,512,3584]{2,1,0:T(8,128)(2,1)S(1)}, bf16[1,512,3584]{2,1,0:T(8,128)(2,1)}, u32[]{:S(2)}) copy-start(bf16[1,512,3584]{2,1,0:T(8,128)(2,1)} %param.10) | copy-start | bytes 11010052
  152.7 86.3 %collective-permute-start = (bf16[512,3584]{1,0:T(8,128)(2,1)}, bf16[512,3584]{1,0:T(8,128)(2,1)}, u32[]{:S(2)}, u32[]{:S(2)}) collective-permute-start(bf16[512,3584]{1,0:T(8,128)(2,1)} %broadcast_select_fusion), channel_id=1, source_target_pairs={{0,1},{1,0},{2,3},{3,2},{4,5},{5,4},{6,7},{7,6},{8,9},{9,8},{10,11... | collective-permute-start | bytes 11010056 | tf_op jit(solution)/shard_map/ppermute | solution.py:244
  238.9 13.1 %copy-start.3 = (s32[16]{0:T(128)S(1)}, s32[16]{0:T(128)}, u32[]{:S(2)}) copy-start(s32[16]{0:T(128)} %param.12) | copy-start | bytes 196
  239.0 13.8 %copy-start.4 = (f32[8]{0:T(128)S(1)}, f32[8]{0:T(128)}, u32[]{:S(2)}) copy-start(f32[8]{0:T(128)} %param.13) | copy-start | bytes 100
  250.1 88.5 %collective-permute-start.1 = (bf16[512,3584]{1,0:T(8,128)(2,1)}, bf16[512,3584]{1,0:T(8,128)(2,1)}, u32[]{:S(2)}, u32[]{:S(2)}) collective-permute-start(bf16[512,3584]{1,0:T(8,128)(2,1)} %get-tuple-element.14.mine), channel_id=1, source_target_pairs={{0,1},{1,0},{2,3},{3,2},{4,5},{5,4},{6,7},{7,6},{8,9},{9,8},{10,11... | collective-permute-start | bytes 11010056 | tf_op jit(solution)/shard_map/ppermute | solution.py:250

commit v3 on v2

--- a/solution.py
+++ b/solution.py
@@ -45,82 +45,132 @@
     return wanted if (rows // 2) % wanted == 0 else 16
 
 
-def spread_kernel(members, ROWS, table, own, out, came, sent, send_sem, recv_sem):
+def spread_kernel(
+    members, height, table, own, out, came, mirror, other, sent,
+    send_sem, recv_sem, near_send, near_recv, back_send, back_recv,
+):
     rows, cols = own.shape
-    blocks = rows // 2 // ROWS
-    steps = blocks + members - 2
+    half = rows // 2
+    blocks = half // height
+    chips = members // 2
+    steps = blocks + chips - 1
     width = cols // PIECES
     place = ring_of(lax.axis_index("pop"), members)
-    ahead = member_at((place + 1) % members, members)
-    behind = member_at((place + members - 1) % members, members)
+    chip = place // 2
+    core = place % 2
+    target = member_at(2 * ((chip + 1 - 2 * core + chips) % chips) + core, members)
+    origin = member_at(2 * ((chip - 1 + 2 * core + chips) % chips) + core, members)
+    partner = member_at(2 * chip + 1 - core, members)
     is_root = table[0] > 0
     chosen = table[1] > 0
-    targets = (ahead, behind)
+    partner_root = table[4] > 0
 
     barrier = pltpu.get_barrier_semaphore()
-    for near in targets:
+    for near in (target, origin, partner):
         pl.semaphore_signal(barrier, inc=1, device_id={"pop": near}, device_id_type=MESH)
-    pl.semaphore_wait(barrier, 2)
-
-    def copy_of(way, step, piece):
-        slot = step % 2
+    pl.semaphore_wait(barrier, 3)
+
+    def block_rows(way, block):
+        return pl.ds(pl.multiple_of(way * half + block * height, height), height)
+
+    def lend(block):
+        return pltpu.make_async_remote_copy(
+            src_ref=own.at[block_rows(1 - core, block), :],
+            dst_ref=other.at[block],
+            send_sem=near_send.at[block],
+            recv_sem=near_recv.at[block],
+            device_id={"pop": partner},
+            device_id_type=MESH,
+        )
+
+    def onward(step, piece):
         cut = pl.ds(piece * width, width)
         return pltpu.make_async_remote_copy(
-            src_ref=sent.at[way, slot, :, cut],
-            dst_ref=came.at[way, step, :, cut],
-            send_sem=send_sem.at[way, slot, piece],
-            recv_sem=recv_sem.at[way, step, piece],
-            device_id={"pop": targets[way]},
+            src_ref=sent.at[step % 2, :, cut],
+            dst_ref=came.at[step, :, cut],
+            send_sem=send_sem.at[step % 2, piece],
+            recv_sem=recv_sem.at[step, piece],
+            device_id={"pop": target},
             device_id_type=MESH,
         )
 
-    def own_rows(way, step):
-        first = way * (rows // 2) + jnp.minimum(step, blocks - 1) * ROWS
-        return pl.ds(pl.multiple_of(first, ROWS), ROWS)
-
+    def across(step):
+        return pltpu.make_async_remote_copy(
+            src_ref=came.at[step],
+            dst_ref=mirror.at[step],
+            send_sem=back_send.at[step],
+            recv_sem=back_recv.at[step],
+            device_id={"pop": partner},
+            device_id_type=MESH,
+        )
+
+    def each(count, act):
+        def body(index, carry):
+            act(index)
+            return carry
+
+        lax.fori_loop(0, count, body, 0)
+
+    each(blocks, lambda block: lend(block).start())
+    lend(0).wait_recv()
     for piece in range(PIECES):
         cut = pl.ds(piece * width, width)
-        for way in range(2):
-            sent[way, 0, :, cut] = own[way * (rows // 2) : way * (rows // 2) + ROWS, cut]
-            copy_of(way, 0, piece).start()
+        sent[0, :, cut] = jnp.where(is_root, own[block_rows(core, 0), cut], other[0, :, cut])
+        onward(0, piece).start()
 
     def forward(step, carry):
+        block = jnp.minimum(step, blocks - 1)
+
+        @pl.when(step < blocks)
+        def _():
+            lend(step).wait_recv()
+
         for piece in range(PIECES):
             cut = pl.ds(piece * width, width)
-            for way in range(2):
-                copy_of(way, step - 1, piece).wait_recv()
-
-                @pl.when(step >= 2)
-                def _():
-                    copy_of(way, step - 2, piece).wait_send()
-
-                sent[way, step % 2, :, cut] = jnp.where(
-                    is_root, own[own_rows(way, step), cut], came[way, step - 1, :, cut]
-                )
-                copy_of(way, step, piece).start()
+            onward(step - 1, piece).wait_recv()
+
+            @pl.when(step >= 2)
+            def _():
+                onward(step - 2, piece).wait_send()
+
+            relayed = jnp.where(partner_root, other[block, :, cut], came[step - 1, :, cut])
+            sent[step % 2, :, cut] = jnp.where(
+                is_root, own[block_rows(core, block), cut], relayed
+            )
+            onward(step, piece).start()
+        across(step - 1).start()
         return carry
 
     lax.fori_loop(1, steps, forward, 0)
     for piece in range(PIECES):
-        for way in range(2):
-            copy_of(way, steps - 1, piece).wait_recv()
-            copy_of(way, steps - 2, piece).wait_send()
-            copy_of(way, steps - 1, piece).wait_send()
-
-    def settle(block, carry):
-        for way in range(2):
-            at = pl.ds(pl.multiple_of(way * (rows // 2) + block * ROWS, ROWS), ROWS)
-            out[at, :] = jnp.where(chosen, came[way, block + table[2 + way]], own[at, :])
-        return carry
-
-    lax.fori_loop(0, blocks, settle, 0)
+        onward(steps - 1, piece).wait_recv()
+    across(steps - 1).start()
+
+    def settle(block):
+        at = block_rows(core, block)
+        out[at, :] = jnp.where(chosen, came[block + table[2 + core]], own[at, :])
+
+    each(blocks, settle)
+    each(steps, lambda step: across(step).wait_recv())
+
+    def settle_other(block):
+        at = block_rows(1 - core, block)
+        out[at, :] = jnp.where(chosen, mirror[block + table[3 - core]], own[at, :])
+
+    each(blocks, settle_other)
+    for piece in range(PIECES):
+        onward(steps - 2, piece).wait_send()
+        onward(steps - 1, piece).wait_send()
+    each(blocks, lambda block: lend(block).wait_send())
+    each(steps, lambda step: across(step).wait_send())
 
 
 def spread(value, table, members, turn, part, parts):
     rows, whole_cols = value.shape
     cols = whole_cols // parts
     height = rows_of(rows, cols, whole_cols)
-    steps = rows // 2 // height + members - 2
+    blocks = rows // 2 // height
+    steps = blocks + members // 2 - 1
     return pl.pallas_call(
         functools.partial(spread_kernel, members, height),
         grid=(1,),
@@ -131,10 +181,16 @@
         ],
         out_specs=pl.BlockSpec((rows, cols), lambda i: (0, 0), pipeline_mode=pl.Buffered(1)),
         scratch_shapes=[
-            pltpu.VMEM((2, steps, height, cols), value.dtype),
-            pltpu.VMEM((2, 2, height, cols), value.dtype),
-            pltpu.SemaphoreType.DMA((2, 2, PIECES)),
-            pltpu.SemaphoreType.DMA((2, steps, PIECES)),
+            pltpu.VMEM((steps, height, cols), value.dtype),
+            pltpu.VMEM((steps, height, cols), value.dtype),
+            pltpu.VMEM((blocks, height, cols), value.dtype),
+            pltpu.VMEM((2, height, cols), value.dtype),
+            pltpu.SemaphoreType.DMA((2, PIECES)),
+            pltpu.SemaphoreType.DMA((steps, PIECES)),
+            pltpu.SemaphoreType.DMA((blocks,)),
+            pltpu.SemaphoreType.DMA((blocks,)),
+            pltpu.SemaphoreType.DMA((steps,)),
+            pltpu.SemaphoreType.DMA((steps,)),
         ],
         compiler_params=pltpu.CompilerParams(
             collective_id=turn, has_side_effects=True, vmem_limit_bytes=60 * 2**20
@@ -207,18 +263,17 @@
     tables = []
     for turn in range(tops):
         root = roots[turn]
-        behind = (place - ring_of(root, members) + members) % members
-        before = (members - behind) % members
-        tables.append(
-            jnp.stack(
-                [
-                    (me == root).astype(jnp.int32),
-                    jnp.logical_and(my_source == root, me != root).astype(jnp.int32),
-                    jnp.maximum(behind - 1, 0).astype(jnp.int32),
-                    jnp.maximum(before - 1, 0).astype(jnp.int32),
-                ]
-            )
-        )
+        chips = members // 2
+        root_place = ring_of(root, members)
+        behind = (place // 2 - root_place // 2 + chips) % chips
+        entries = (
+            me == root,
+            jnp.logical_and(my_source == root, me != root),
+            (behind + chips - 1) % chips,
+            (2 * chips - behind - 1) % chips,
+            jnp.logical_and(place // 2 == root_place // 2, me != root),
+        )
+        tables.append(jnp.stack([entry.astype(jnp.int32) for entry in entries]))
 
     def take(value, first, part=0, parts=1):
         taken = None

time: 363 us -> 358 us (0.986)
  Pallas kernels: 321 us -> 313 us
    pallas_call x3, Pallas kernels: 297 us -> 289 us  [spread(): pl.pallas_call(functools.partial(spread_kernel, members, height), grid=(1...]
  transfers between devices with their start and end apart: 2 -> 2, of which waited for: 0 -> 1; matrix products, arithmetic and copies ran while one was open for 1% -> 1% of each run, Pallas kernels for 47% -> 44%
where the time goes in v3:
time: 358 us; the launch traced here: 357 us
  Pallas kernels  313 us (87%)
  other arithmetic  19.3 us (5%)
  matrix products  12.6 us (4%)
  local copies, waits for them, and re-layouts  5.81 us (2%)
    pallas_call x3, Pallas kernels, spread(): pl.pallas_call(functools.partial(spread_kernel, members, height), grid=(1...  289 us
    pallas_call x1, Pallas kernels, update(): pl.pallas_call(functools.partial(update_kernel, half), grid_spec=pltpu.Pr...  23.8 us
    dot_general x1, matrix products, local(): jnp.dot(inputs, taken_weight, preferred_element_type=jnp.float32)  12.6 us
    convert_element_type x1, other arithmetic, activate(): pullback(cot_block.astype(jnp.float32))[0].astype(jnp.bfloat16)  11.1 us
  transfers between devices with their start and end apart: 2, of which 1 were waited for; matrix products, arithmetic and copies ran while one was open for 1% of the time, Pallas kernels for 44%

profile of v3, /device:TPU:1, one launch (start us, length us, event | category | flops | bytes accessed | tf_op | source)
XLA Modules:
  0.0 357.0 jit_solution(18082342619001053336)
XLA Ops:
  0.7 1.4 fusion.16
  2.1 1.3 compare_reduce_fusion
  3.4 0.7 slice_bitcast_fusion
  4.1 0.1 fusion.13
  4.2 1.2 sort.15
  7.0 0.6 stack.35.table
  7.6 132.4 %spread_0.1.weight = bf16[896,7168]{1,0:T(8,128)(2,1)} custom-call(s32[5]{0:T(128)} %stack.35.table, bf16[896,7168]{1,0:T(8,128)(2,1)} %bitcast.37), custom_call_target="tpu_custom_call" | custom-call | bytes 314572800 | tf_op jit(solution)/shard_map/spread_0/pallas_call | solution.py:174
  140.0 12.6 %fusion = bf16[512,7168]{1,0:T(8,128)(2,1)S(1)} fusion(bf16[896,7168]{1,0:T(8,128)(2,1)} %spread_0.1.weight, bf16[1,512,896]{2,1,0:T(8,128)(2,1)S(1)} %copy-done.2), kind=kOutput, calls=%fused_computation.3 | convolution fusion | flops 6580338688 | bytes 21102592 | tf_op jit(solution)/shard_map/dot_general | solution.py:291
  152.7 0.0 copy-start
  152.7 3.0 copy-done
  155.7 2.2 broadcast_select_fusion
  157.9 1.2 collective-permute-start
  159.1 78.3 %spread_1.1.first = bf16[896,3584]{1,0:T(8,128)(2,1)} custom-call(s32[5]{0:T(128)} %stack.35.table, bf16[896,7168]{1,0:T(8,128)(2,1)} %bitcast.35), custom_call_target="tpu_custom_call" | custom-call | bytes 157286400 | tf_op jit(solution)/shard_map/spread_1/pallas_call | solution.py:174
  237.5 0.0 copy-start.3
  237.5 0.0 copy-start.4
  237.5 1.6 collective-permute-done
  239.1 11.1 %fusion.3 = (bf16[512,3584]{1,0:T(8,128)(2,1)}, bf16[1,512,3584]{2,1,0:T(8,128)(2,1)}) fusion(bf16[512,3584]{1,0:T(8,128)(2,1)} %collective-permute-done, bf16[1,512,3584]{2,1,0:T(8,128)(2,1)S(1)} %copy-done.1, bf16[512,7168]{1,0:T(8,128)(2,1)} %copy-done, pred[]{:T(512)S(6)} %eq.57), kind=kLoop, calls=%fused_computation.8 | loop fusion | flops 49545216 | bytes 22020096 | tf_op jit(solution)/shard_map/convert_element_type | solution.py:39
  250.2 1.2 collective-permute-start.1
  251.4 1.5 copy.11
  252.9 0.6 fusion.14
  253.5 1.2 fusion.15
  254.8 78.4 %spread_2.1.second = bf16[896,3584]{1,0:T(8,128)(2,1)} custom-call(s32[5]{0:T(128)} %stack.35.table, bf16[896,7168]{1,0:T(8,128)(2,1)} %bitcast.36), custom_call_target="tpu_custom_call" | custom-call | bytes 157286400 | tf_op jit(solution)/shard_map/spread_2/pallas_call | solution.py:174
  333.2 0.0 collective-permute-done.1.theirs
  333.2 23.8 %update.1 = bf16[896,7168]{1,0:T(8,128)(2,1)} custom-call(s32[1]{0:T(128)} %bitcast.13.side, f32[1]{0:T(128)} %bitcast.14.rate, bf16[896,512]{1,0:T(8,128)(2,1)S(1)} %bitcast.34, bf16[512,3584]{1,0:T(8,128)(2,1)} %get-tuple-element.14.mine, bf16[512,3584]{1,0:T(8,128)(2,1)} %collective-permute-done.1.theirs, bf16[896,7168]{1,0:T(8,128)(2,1)} %spread_0.1.weight, ...), custom_call_target="tpu_custom_call" | custom-call | flops 6576668672 | bytes 38535168 | tf_op jit(solution)/shard_map/update/pallas_call | solution.py:220
  (8 shorter events, 0.0 us)
Async XLA Ops:
  7.6 132.4 %copy-start.2 = (bf16[1,512,896]{2,1,0:T(8,128)(2,1)S(1)}, bf16[1,512,896]{2,1,0:T(8,128)(2,1)}, u32[]{:S(2)}) copy-start(bf16[1,512,896]{2,1,0:T(8,128)(2,1)} %param.7) | copy-start | bytes 2752516
  152.7 3.1 copy-start
  157.9 81.2 %copy-start.1 = (bf16[1,512,3584]{2,1,0:T(8,128)(2,1)S(1)}, bf16[1,512,3584]{2,1,0:T(8,128)(2,1)}, u32[]{:S(2)}) copy-start(bf16[1,512,3584]{2,1,0:T(8,128)(2,1)} %param.10) | copy-start | bytes 11010052
  157.9 81.2 %collective-permute-start = (bf16[512,3584]{1,0:T(8,128)(2,1)}, bf16[512,3584]{1,0:T(8,128)(2,1)}, u32[]{:S(2)}, u32[]{:S(2)}) collective-permute-start(bf16[512,3584]{1,0:T(8,128)(2,1)} %broadcast_select_fusion), channel_id=1, source_target_pairs={{0,1},{1,0},{2,3},{3,2},{4,5},{5,4},{6,7},{7,6},{8,9},{9,8},{10,11... | collective-permute-start | bytes 11010056 | tf_op jit(solution)/shard_map/ppermute | solution.py:299
  237.5 15.4 %copy-start.3 = (s32[16]{0:T(128)S(1)}, s32[16]{0:T(128)}, u32[]{:S(2)}) copy-start(s32[16]{0:T(128)} %param.12) | copy-start | bytes 196
  237.5 16.0 %copy-start.4 = (f32[8]{0:T(128)S(1)}, f32[8]{0:T(128)}, u32[]{:S(2)}) copy-start(f32[8]{0:T(128)} %param.13) | copy-start | bytes 100
  250.2 83.0 %collective-permute-start.1 = (bf16[512,3584]{1,0:T(8,128)(2,1)}, bf16[512,3584]{1,0:T(8,128)(2,1)}, u32[]{:S(2)}, u32[]{:S(2)}) collective-permute-start(bf16[512,3584]{1,0:T(8,128)(2,1)} %get-tuple-element.14.mine), channel_id=1, source_target_pairs={{0,1},{1,0},{2,3},{3,2},{4,5},{5,4},{6,7},{7,6},{8,9},{9,8},{10,11... | collective-permute-start | bytes 11010056 | tf_op jit(solution)/shard_map/ppermute | solution.py:305
